TPU v7x, 256 devices: a whole 4x4x8 slice. The times are simulated.
256 devices in a mesh: dp: 8 (over z_lo, core), seq: 16 (over x, y), mp: 2 (over z_hi).
Axes of the slice: x: 4, y: 4, z: 8 (z_hi: 2, z_lo: 4; z = z_hi * 4 + z_lo), core: 2. Of those that a mesh axis runs over, the one named last changes fastest.
Arguments:
- features: bfloat16 [8, 8192, 1408], P('dp', ('seq', 'mp')), may hold values from -6 to 6
- conv_weight: bfloat16 [5, 1408, 1536], P(None, ('seq', 'mp')), may hold values from -0.0625 to 0.0625
- norm_gain: float32 [1536], replicated, may hold values from 0.25 to 1.75
- query_weight: bfloat16 [1536, 1024], replicated, may hold values from -0.15625 to 0.15625
- keyval_weight: bfloat16 [1536, 320], replicated, may hold values from -0.15625 to 0.15625
- head_scale: float32 [8], replicated, may hold values from 0.5 to 24
- output_weight: bfloat16 [1536, 1536], replicated, may hold values from -0.15625 to 0.15625
- pair_weight: bfloat16 [1536, 256], replicated, may hold values from -0.625 to 0.625
- pair_input: bfloat16 [8, 256, 256, 128], P('dp', ('seq', 'mp')), may hold values from -6 to 6
- flip_weight: bfloat16 [128, 128], replicated, may hold values from -0.5 to 0.5
- pair_cotangent: bfloat16 [8, 256, 256, 128], P('dp', ('seq', 'mp')), may hold values from -0.0234375 to 0.0234375
Outputs:
- block_out: bfloat16 [8, 4096, 1536], P('dp', ('seq', 'mp'))
- pair_out: bfloat16 [8, 256, 256, 128], P('dp', ('seq', 'mp'))
- grad_flip: float32 [128, 128], replicated
All inputs are finite; a program needn't handle non-finite values.
Results may differ from a plain program's by a relative error of at most 0.011.
Values may be sent and summed in bfloat16 or wider, within the bound.
A program may use at most 192 MiB of HBM per device.

v0:
```python
import math
import jax
import jax.numpy as jnp
from jax import lax
from jax.sharding import PartitionSpec as P

PAIR_POOL = 16
norm_eps = 1e-06
logit_cap = 50.0


def padded_2(shard, sides, width):
    for axis, dim in sides:
        devices, length = (lax.axis_size(axis), shard.shape[dim])
        up = [(i, (i + 1) % devices) for i in range(devices - 1)]
        down = [(j, i) for i, j in up]
        last = lax.slice_in_dim(shard, length - width, length, axis=dim)
        initial = lax.slice_in_dim(shard, 0, width, axis=dim)
        before = lax.ppermute(last, axis, up)
        after = lax.ppermute(initial, axis, down)
        shard = jnp.concatenate([before, shard, after], axis=dim)
    return shard


def root_norm(values_in):
    return values_in * lax.rsqrt(jnp.mean(values_in * values_in, axis=-1, keepdims=True) + norm_eps)


def prepare(raw):
    return jax.nn.gelu(root_norm(raw.astype(jnp.float32)), approximate=False).astype(jnp.bfloat16)


def tap_sum(source, out_rows, tap_count, running, filter_rows):
    for lag_index in range(tap_count):
        running = running + jnp.dot(
            source[lag_index : lag_index + out_rows],
            filter_rows[lag_index],
            preferred_element_type=jnp.float32,
        )
    return running


def per_device(
    features,
    conv_weight,
    norm_gain,
    query_weight,
    keyval_weight,
    head_scale,
    output_weight,
    pair_weight,
    pair_input,
    flip_weight,
    pair_cotangent,
):
    fine_rows = features.shape[1]
    coarse_rows = fine_rows // 2
    in_channels = features.shape[2]
    model_dim = output_weight.shape[1]
    head_count = head_scale.shape[0]
    key_dim = query_weight.shape[1] // head_count
    pair_dim = flip_weight.shape[0]
    tap_count = conv_weight.shape[0]
    margin = tap_count // 2
    padded = padded_2(features, ((("seq", "mp"), 1),), margin)
    prepared = prepare(padded[0])
    starting = jnp.zeros((fine_rows, model_dim), jnp.float32)
    conv_sum = tap_sum(
        prepared,
        fine_rows,
        tap_count,
        starting,
        lax.all_gather(conv_weight, ("seq", "mp"), axis=1, tiled=True),
    )
    skipped = jnp.pad(features[0].astype(jnp.float32), ((0, 0), (0, model_dim - in_channels)))
    encoded = jnp.max((conv_sum + skipped).reshape(coarse_rows, 2, model_dim), axis=1).astype(
        jnp.bfloat16
    )
    widened = encoded.astype(jnp.float32)
    normed = (root_norm(widened) * norm_gain).astype(jnp.bfloat16)
    scale_row = jnp.repeat(head_scale, key_dim) / math.sqrt(key_dim)
    queries = (
        jnp.dot(normed, query_weight, preferred_element_type=jnp.float32) * scale_row
    ).astype(jnp.bfloat16)
    keyvals = jnp.dot(normed, keyval_weight, preferred_element_type=jnp.float32).astype(
        jnp.bfloat16
    )
    pooled = jnp.mean(
        widened.reshape(coarse_rows // PAIR_POOL, PAIR_POOL, model_dim), axis=1
    ).astype(jnp.bfloat16)
    pair_feats = jnp.dot(pooled, pair_weight, preferred_element_type=jnp.float32).astype(
        jnp.bfloat16
    )
    pair_q = pair_feats[:, :pair_dim]
    pair_k = pair_feats[:, pair_dim:]
    keys_all, pairk_all = (
        lax.all_gather(keyvals[None], ("seq", "mp"), axis=1, tiled=True),
        lax.all_gather(pair_k[None], ("seq", "mp"), axis=1, tiled=True),
    )
    summed = (
        pair_input[0].astype(jnp.float32)
        + pair_q[:, None, :].astype(jnp.float32) * pairk_all[0][None, :, :].astype(jnp.float32)
    ).astype(jnp.bfloat16)
    flipped = lax.all_to_all(summed[None], ("seq", "mp"), split_axis=2, concat_axis=1, tiled=True)[
        0
    ]
    turned = jnp.einsum("bac,cd->abd", flipped, flip_weight, preferred_element_type=jnp.float32)
    pair_out = (summed.astype(jnp.float32) + turned).astype(jnp.bfloat16)
    grad_term = jnp.einsum(
        "bac,abd->cd", flipped, pair_cotangent[0], preferred_element_type=jnp.float32
    )
    grad_flip = lax.psum(grad_term, ("dp", "seq", "mp"))
    key_rows = keys_all[0][:, :key_dim]
    value_rows = keys_all[0][:, key_dim:]
    query_rows = queries.reshape(coarse_rows * head_count, key_dim)
    scores = jnp.dot(query_rows, key_rows.T, preferred_element_type=jnp.float32)
    weights = jnp.exp(logit_cap * jnp.tanh(scores / logit_cap))
    totals = jnp.sum(weights, axis=-1, keepdims=True)
    mixed = (
        jnp.dot(weights.astype(jnp.bfloat16), value_rows, preferred_element_type=jnp.float32)
        / totals
    )
    heads_out = mixed.astype(jnp.bfloat16).reshape(coarse_rows, head_count * value_rows.shape[1])
    block_out = (
        widened + jnp.dot(heads_out, output_weight, preferred_element_type=jnp.float32)
    ).astype(jnp.bfloat16)
    return (block_out[None], pair_out[None], grad_flip)


def solution(mesh):
    placed = (
        P("dp", ("seq", "mp"), None),
        P(None, ("seq", "mp"), None),
        P(),
        P(),
        P(),
        P(),
        P(),
        P(),
        P("dp", ("seq", "mp"), None, None),
        P(),
        P("dp", ("seq", "mp"), None, None),
    )
    return jax.shard_map(
        per_device,
        mesh=mesh,
        in_specs=placed,
        out_specs=(P("dp", ("seq", "mp"), None), P("dp", ("seq", "mp"), None, None), P()),
        check_vma=False,
    )
```

profile of v0, /device:TPU:1, one launch (start us, length us, event | category | flops | bytes accessed | tf_op | source)
XLA Modules:
  0.0 959.2 jit_solution(9439417309653292819)
XLA Ops:
  7.2 2.7 copy.24
  10.0 0.8 fusion.84
  10.7 1.3 collective-permute-start.1
  12.0 10.3 %collective-permute-start = (bf16[1,2,1408]{2,1,0:T(2,128)(2,1)S(1)}, bf16[1,2,1408]{2,1,0:T(2,128)(2,1)S(1)}, u32[]{:S(2)}, u32[]{:S(2)}) collective-permute-start(bf16[1,2,1408]{2,1,0:T(2,128)(2,1)S(1)} %get-tuple-element.8), channel_id=1, source_target_pairs={{0,1},{1,2},{2,3},{3,4},{4,5},{5,6},{6,7},{7,8},{8,9},{9,10},{10,1... | collective-permute-start | bytes 16904 | tf_op jit(solution)/shard_map/ppermute | solution.py:19
  23.1 1.4 fusion.48
  24.5 6.0 fusion.20
  30.5 426.3 %all-gather.5.cloned.1.call-done = bf16[5,1408,1536]{2,0,1:T(8,128)(2,1)} async-done(((bf16[5,44,1536]{2,0,1:T(8,128)(2,1)}), bf16[5,1408,1536]{2,0,1:T(8,128)(2,1)}) %all-gather.5.cloned.1.call-update) | async-done | bytes 21626896 | tf_op jit(solution)/shard_map/all_gather | solution.py:73
  456.8 92.6 %fusion.83 = (bf16[1,1408,1536]{2,0,1:T(2,128)(2,1)S(1)}, bf16[1,1408,1536]{2,0,1:T(2,128)(2,1)S(1)}, bf16[1,1408,1536]{2,0,1:T(2,128)(2,1)}, bf16[1,1408,1536]{2,0,1:T(2,128)(2,1)}, bf16[1,1408,1536]{2,0,1:T(2,128)(2,1)}) fusion(bf16[5,1408,1536]{2,0,1:T(8,128)(2,1)} %all-gather.5.cloned.1.call-done), kind=kLoop, calls=%fused_computation.101 | loop fusion | bytes 43253760 | tf_op jit(solution)/shard_map/slice | solution.py:37
  549.4 5.0 fusion.7
  554.5 4.9 fusion.9
  559.4 1.4 fusion.10
  560.8 1.4 fusion.11
  562.3 2.3 fusion.13
  564.6 2.9 reshape.58
  567.5 3.0 reduce_max.9
  570.7 2.3 convolution_convert_fusion
  573.2 1.4 convolution_convert_fusion.1
  574.6 105.2 %all-gather.1 = bf16[256,128]{1,0:T(8,128)(2,1)S(1)} all-gather(bf16[8,128]{1,0:T(8,128)(2,1)S(1)} %get-tuple-element.11), channel_id=3, replica_groups=mesh['dp'=8,'seq'=16,'mp'=2] {'seq','mp'}, dimensions={0}, use_global_device_ids=true | all-gather | bytes 67584 | tf_op jit(solution)/shard_map/all_gather | solution.py:98
  680.5 1.1 copy.31
  681.6 4.6 all-to-all-start
  687.0 1.3 fusion.52
  688.3 1.8 reshape.59
  690.1 9.7 %all-to-all-done = bf16[1,8,256,128]{3,1,0,2:T(8,128)(2,1)} async-done(((bf16[1,8,256,128]{3,1,0,2:T(8,128)(2,1)}), bf16[1,8,256,128]{3,1,0,2:T(8,128)(2,1)}, u32[]{:S(2)}, u32[]{:S(2)}) %all-to-all-start) | async-done | bytes 524320 | tf_op jit(solution)/shard_map/all_to_all | solution.py:104
  699.8 2.2 convolution_bitcast_fusion.1
  702.0 2.3 fusion.51
  704.4 6.7 fusion
  711.1 5.9 fusion.63
  717.0 2.0 copy.30
  719.0 2.3 reshape.60
  721.3 4.0 fusion.15
  725.3 225.9 %all-reduce.3.cloned.1.call-done = f32[128,128]{1,0:T(8,128)} async-done(((f32[128,128]{1,0:T(8,128)}), f32[128,128]{1,0:T(8,128)}) %all-reduce.3.cloned.1.call-update) | async-done | bytes 65552 | tf_op jit(solution)/shard_map/psum | solution.py:112
  951.2 1.5 copy.69
  (39 shorter events, 2.7 us)
Async XLA Ops:
  7.2 679.8 %copy-start = (bf16[1536,1024]{1,0:T(8,128)(2,1)S(1)}, bf16[1536,1024]{1,0:T(8,128)(2,1)}, u32[]{:S(2)}) copy-start(bf16[1536,1024]{1,0:T(8,128)(2,1)} %param.14) | copy-start | bytes 9437188
  7.2 449.6 %all-gather.5.cloned.1.call-start = ((), (), s32[]{:S(2)}) async-start(), calls=%async_computation.1 | async-start | bytes 35684352 | tf_op jit(solution)/shard_map/all_gather | solution.py:73
  9.9 694.5 %all-gather.7.cloned.1.call-start = ((), (), s32[]{:S(2)}) async-start(), calls=%async_computation.3 | async-start | bytes 2703360 | tf_op jit(solution)/shard_map/all_gather | solution.py:97
  10.7 11.6 %collective-permute-start.1 = (bf16[1,2,1408]{2,1,0:T(2,128)(2,1)S(1)}, bf16[1,2,1408]{2,1,0:T(2,128)(2,1)S(1)}, u32[]{:S(2)}, u32[]{:S(2)}) collective-permute-start(bf16[1,2,1408]{2,1,0:T(2,128)(2,1)S(1)} %get-tuple-element.9), channel_id=1, source_target_pairs={{1,0},{2,1},{3,2},{4,3},{5,4},{6,5},{7,6},{8,7},{9,8},{10,9},{11,1... | collective-permute-start | bytes 16904 | tf_op jit(solution)/shard_map/ppermute | solution.py:20
  12.0 11.0 %collective-permute-start = (bf16[1,2,1408]{2,1,0:T(2,128)(2,1)S(1)}, bf16[1,2,1408]{2,1,0:T(2,128)(2,1)S(1)}, u32[]{:S(2)}, u32[]{:S(2)}) collective-permute-start(bf16[1,2,1408]{2,1,0:T(2,128)(2,1)S(1)} %get-tuple-element.8), channel_id=1, source_target_pairs={{0,1},{1,2},{2,3},{3,4},{4,5},{5,6},{6,7},{7,8},{8,9},{9,10},{10,1... | collective-permute-start | bytes 16904 | tf_op jit(solution)/shard_map/ppermute | solution.py:19
  456.8 92.6 %copy-start.4 = (bf16[260,1408]{1,0:T(8,128)(2,1)S(1)}, bf16[260,1408]{1,0:T(8,128)(2,1)}, u32[]{:S(2)}) copy-start(bf16[260,1408]{1,0:T(8,128)(2,1)} %fusion.20) | copy-start | bytes 2196484
  549.4 9.9 %slice-start = ((s8[8650752]{0:T(1024)(128)(4,1)}), s8[4194304]{0:T(1024)(128)(4,1)S(1)}, s32[]{:S(2)}) async-start(s8[8650752]{0:T(1024)(128)(4,1)} %bitcast.79), calls=%async_computation.4 | async-start | bytes 8388608
  549.4 9.9 %slice-start.1 = ((s8[8650752]{0:T(1024)(128)(4,1)}), s8[4194304]{0:T(1024)(128)(4,1)S(1)}, s32[]{:S(2)}) async-start(s8[8650752]{0:T(1024)(128)(4,1)} %bitcast.79), calls=%async_computation.5 | async-start | bytes 8388608
  554.4 4.9 slice-start.2
  560.8 1.4 copy-start.1
  564.6 6.1 copy-start.5
  573.0 106.8 %copy-start.2 = (bf16[1,8,256,128]{3,2,1,0:T(8,128)(2,1)S(1)}, bf16[1,8,256,128]{3,2,1,0:T(8,128)(2,1)}, u32[]{:S(2)}) copy-start(bf16[1,8,256,128]{3,2,1,0:T(8,128)(2,1)} %param.19) | copy-start | bytes 1572868
  679.8 0.6 copy-start.3
  681.6 18.2 %all-to-all-start = ((bf16[1,8,256,128]{3,1,0,2:T(8,128)(2,1)}), bf16[1,8,256,128]{3,1,0,2:T(8,128)(2,1)}, u32[]{:S(2)}, u32[]{:S(2)}) async-start(bf16[1,8,256,128]{3,1,0,2:T(8,128)(2,1)} %copy.31), calls=%async_computation | async-start | bytes 1048576 | tf_op jit(solution)/shard_map/all_to_all | solution.py:104
  686.2 264.9 %all-reduce.3.cloned.1.call-start = ((), (), s32[]{:S(2)}) async-start(), calls=%async_computation.2 | async-start | bytes 131072 | tf_op jit(solution)/shard_map/psum | solution.py:112
  704.4 6.7 copy-start.6
Sparse Core Ops, SparseCore 0:
  11.4 445.3 all-gather.4
  573.2 103.0 all-gather.6
  704.5 246.6 all-reduce.2
where the time goes:
time: 960 us; the launch traced here: 959 us
  waiting for transfers between devices  663 us (69%)
  local copies, waits for them, and re-layouts  108 us (11%)
  blocking collectives  105 us (11%)
  matrix products  41.2 us (4%)
  starting transfers between devices  16.3 us (2%)
  between operations  14 us (1%)
  other arithmetic  11.6 us (1%)
    all_gather x1, waiting for transfers between devices, per_device(): lax.all_gather(conv_weight, ('seq', 'mp'), axis=1, tiled=True)  426 us
    psum x1, waiting for transfers between devices, per_device(): grad_flip = lax.psum(grad_term, ('dp', 'seq', 'mp'))  226 us
    all_gather x1, blocking collectives, per_device(): lax.all_gather(pair_k[None], ('seq', 'mp'), axis=1, tiled=True)  105 us
    slice x1, local copies, waits for them, and re-layouts, tap_sum(): filter_rows[lag_index]  92.6 us
  transfers between devices with their start and end apart: 6, of which 4 were waited for; matrix products, arithmetic and copies ran while one was open for 4% of the time, Pallas kernels for 0%

commit v1 on v0

--- a/solution.py
+++ b/solution.py
@@ -109,7 +109,7 @@
     grad_term = jnp.einsum(
         "bac,abd->cd", flipped, pair_cotangent[0], preferred_element_type=jnp.float32
     )
-    grad_flip = lax.psum(grad_term, ("dp", "seq", "mp"))
+    grad_flip = jnp.sum(lax.all_gather(grad_term, ("dp", "seq", "mp")), axis=0)
     key_rows = keys_all[0][:, :key_dim]
     value_rows = keys_all[0][:, key_dim:]
     query_rows = queries.reshape(coarse_rows * head_count, key_dim)

time: 960 us -> 1460 us (1.52)
  waiting for transfers between devices: 663 us -> 1140 us
  blocking collectives: 105 us -> 125 us
    all_gather x0 -> x1, waiting for transfers between devices: none -> 713 us  [per_device(): grad_flip = jnp.sum(lax.all_gather(grad_term, ('dp', 'seq', 'mp')), axis=0)]
    psum x1 -> x0, waiting for transfers between devices: 226 us -> none  [per_device(): grad_flip = lax.psum(grad_term, ('dp', 'seq', 'mp'))]
    all_to_all x0 -> x1, blocking collectives: none -> 16.6 us  [per_device(): lax.all_to_all(summed[None], ('seq', 'mp'), split_axis=2, concat_axis=1,...]
  transfers between devices with their start and end apart: 6 -> 5, of which waited for: 4 -> 3; matrix products, arithmetic and copies ran while one was open for 4% -> 3% of each run, Pallas kernels for 0% -> 0%
where the time goes in v1:
time: 1460 us
  waiting for transfers between devices  1140 us (78%)
  blocking collectives  125 us (9%)
  local copies, waits for them, and re-layouts  106 us (7%)
  matrix products  40 us (3%)
  other arithmetic  18.8 us (1%)
    all_gather x1, waiting for transfers between devices, per_device(): grad_flip = jnp.sum(lax.all_gather(grad_term, ('dp', 'seq', 'mp')), axis=0)  713 us
    all_gather x1, waiting for transfers between devices, per_device(): lax.all_gather(conv_weight, ('seq', 'mp'), axis=1, tiled=True)  426 us
    all_gather x1, blocking collectives, per_device(): lax.all_gather(pair_k[None], ('seq', 'mp'), axis=1, tiled=True)  108 us
    slice x1, local copies, waits for them, and re-layouts, tap_sum(): filter_rows[lag_index]  92.6 us
  transfers between devices with their start and end apart: 5, of which 3 were waited for; matrix products, arithmetic and copies ran while one was open for 3% of the time, Pallas kernels for 0%

profile of v1, /device:TPU:1, one launch (start us, length us, event | category | flops | bytes accessed | tf_op | source)
XLA Modules:
  0.0 1455.5 jit_solution(18303395627275141844)
XLA Ops:
  7.2 2.7 copy.24
  10.0 0.8 fusion.84
  10.7 1.3 collective-permute-start.1
  12.0 10.3 collective-permute-start
  22.3 0.7 collective-permute-done
  23.1 1.4 fusion.48
  24.5 6.0 fusion.20
  30.5 426.3 %all-gather.7.cloned.1.call-done = bf16[5,1408,1536]{2,0,1:T(8,128)(2,1)} async-done(((bf16[5,44,1536]{2,0,1:T(8,128)(2,1)}), bf16[5,1408,1536]{2,0,1:T(8,128)(2,1)}) %all-gather.7.cloned.1.call-update) | async-done | bytes 21626896 | tf_op jit(solution)/shard_map/all_gather | solution.py:73
  456.8 92.6 %fusion.83 = (bf16[1,1408,1536]{2,0,1:T(2,128)(2,1)S(1)}, bf16[1,1408,1536]{2,0,1:T(2,128)(2,1)S(1)}, bf16[1,1408,1536]{2,0,1:T(2,128)(2,1)}, bf16[1,1408,1536]{2,0,1:T(2,128)(2,1)}, bf16[1,1408,1536]{2,0,1:T(2,128)(2,1)}) fusion(bf16[5,1408,1536]{2,0,1:T(8,128)(2,1)} %all-gather.7.cloned.1.call-done), kind=kLoop, calls=%fused_computation.101 | loop fusion | bytes 43253760 | tf_op jit(solution)/shard_map/slice | solution.py:37
  549.4 5.0 fusion.7
  554.5 4.9 fusion.9
  559.4 1.4 fusion.10
  560.8 1.4 fusion.11
  562.3 2.3 fusion.13
  564.6 2.9 reshape.58
  567.5 3.0 reduce_max.9
  570.7 2.3 convolution_convert_fusion
  573.2 1.4 convolution_convert_fusion.1
  574.6 108.1 %all-gather.1 = bf16[256,128]{1,0:T(8,128)(2,1)S(1)} all-gather(bf16[8,128]{1,0:T(8,128)(2,1)S(1)} %get-tuple-element.11), channel_id=3, replica_groups=mesh['dp'=8,'seq'=16,'mp'=2] {'seq','mp'}, dimensions={0}, use_global_device_ids=true | all-gather | bytes 67584 | tf_op jit(solution)/shard_map/all_gather | solution.py:98
  683.3 16.6 %all_to_all.15 = bf16[1,8,256,128]{3,1,0,2:T(8,128)(2,1)S(1)} all-to-all(bf16[1,8,256,128]{3,1,0,2:T(8,128)(2,1)S(1)} %copy.31), channel_id=1, replica_groups=mesh['dp'=8,'seq'=16,'mp'=2] {'seq','mp'}, dimensions={2} | all-to-all | bytes 1048576 | tf_op jit(solution)/shard_map/all_to_all | solution.py:104
  699.9 0.8 copy-done.1
  700.7 1.0 convolution_bitcast_fusion.1
  702.5 1.3 fusion.52
  703.8 1.8 reshape.59
  705.5 2.3 fusion.51
  707.9 6.7 fusion
  714.6 5.9 fusion.63
  720.5 2.0 copy.30
  722.5 2.3 reshape.60
  724.8 4.0 fusion.15
  728.8 713.0 %all-gather.11.cloned.1.call-done = f32[32768,128]{1,0:T(8,128)} async-done(((f32[128,128]{1,0:T(8,128)}), f32[32768,128]{1,0:T(8,128)}) %all-gather.11.cloned.1.call-update) | async-done | bytes 16777232 | tf_op jit(solution)/shard_map/all_gather | solution.py:112
  1441.8 7.2 reduce_sum.49
  (42 shorter events, 1.8 us)
Async XLA Ops:
  7.2 695.3 %copy-start = (bf16[1536,1024]{1,0:T(8,128)(2,1)S(1)}, bf16[1536,1024]{1,0:T(8,128)(2,1)}, u32[]{:S(2)}) copy-start(bf16[1536,1024]{1,0:T(8,128)(2,1)} %param.14) | copy-start | bytes 9437188
  7.2 449.6 %all-gather.7.cloned.1.call-start = ((), (), s32[]{:S(2)}) async-start(), calls=%async_computation.1 | async-start | bytes 35684352 | tf_op jit(solution)/shard_map/all_gather | solution.py:73
  9.9 698.0 %all-gather.9.cloned.1.call-start = ((), (), s32[]{:S(2)}) async-start(), calls=%async_computation.2 | async-start | bytes 2703360 | tf_op jit(solution)/shard_map/all_gather | solution.py:97
  10.7 11.6 collective-permute-start.1
  12.0 11.0 collective-permute-start
  456.8 92.6 %copy-start.5 = (bf16[260,1408]{1,0:T(8,128)(2,1)S(1)}, bf16[260,1408]{1,0:T(8,128)(2,1)}, u32[]{:S(2)}) copy-start(bf16[260,1408]{1,0:T(8,128)(2,1)} %fusion.20) | copy-start | bytes 2196484
  549.4 9.9 slice-start
  549.4 9.9 slice-start.1
  554.4 4.9 slice-start.2
  560.8 1.4 copy-start.2
  564.6 6.1 copy-start.7
  573.0 868.7 %all-gather.11.cloned.1.call-start = ((), (), s32[]{:S(2)}) async-start(), calls=%async_computation.3 | async-start | bytes 16842752 | tf_op jit(solution)/shard_map/all_gather | solution.py:112
  573.1 109.7 %copy-start.3 = (bf16[1,8,256,128]{3,2,1,0:T(8,128)(2,1)S(1)}, bf16[1,8,256,128]{3,2,1,0:T(8,128)(2,1)}, u32[]{:S(2)}) copy-start(bf16[1,8,256,128]{3,2,1,0:T(8,128)(2,1)} %param.19) | copy-start | bytes 1572868
  682.7 17.2 %copy-start.4 = (f32[256,128]{1,0:T(8,128)}, f32[256,128]{1,0:T(8,128)S(1)}, u32[]{:S(2)}) copy-start(f32[256,128]{1,0:T(8,128)S(1)} %mul.112) | copy-start | bytes 393220
  682.7 18.0 %copy-start.6 = (bf16[1,8,256,128]{3,2,1,0:T(8,128)(2,1)S(1)}, bf16[1,8,256,128]{3,2,1,0:T(8,128)(2,1)}, u32[]{:S(2)}) copy-start(bf16[1,8,256,128]{3,2,1,0:T(8,128)(2,1)} %param.21) | copy-start | bytes 1572868
  699.9 0.8 copy-start.1
  707.9 6.7 copy-start.8
Sparse Core Ops, SparseCore 0:
  11.4 445.3 all-gather.6
  573.2 104.7 all-gather.8
  701.8 739.8 all-gather.10
